TPU v7x, 512 devices: a whole 4x4x16 slice. The times are simulated.
512 devices in a mesh: dp: 8 (over y, core), ctx: 64 (over z, x).
Axes of the slice: x: 4, y: 4, z: 16, core: 2. Of those that a mesh axis runs over, the one named last changes fastest.
Arguments:
- query_in: bfloat16 [8, 8192, 1792], P('dp', 'ctx'), may hold values from -8 to 8
- key_in: bfloat16 [8, 8192, 256], P('dp', 'ctx'), may hold values from -4 to 4
- value_input: bfloat16 [8, 8192, 256], P('dp', 'ctx'), may hold values from -4 to 4
- output_gradient: bfloat16 [8, 8192, 1792], P('dp', 'ctx'), may hold values from -5 to 5
- doc_ids: int32 [8, 8192], P('dp', 'ctx'), may hold values from 0 to 1, as said below
- query_bias: float32 [1792], replicated, may hold values from -2 to 2
Outputs:
- attended: bfloat16 [8, 8192, 1792], P('dp', 'ctx')
- grad_query: bfloat16 [8, 8192, 1792], P('dp', 'ctx')
- key_gradient: bfloat16 [8, 8192, 256], P('dp', 'ctx')
- value_gradient: bfloat16 [8, 8192, 256], P('dp', 'ctx')
- grad_bias: float32 [1792], replicated
Inputs may be any that keep to these rules, and one draw needn't show every extreme that they name: `doc_ids`: ids never fall along a sequence; each of the 2 documents of a sequence holds 2048 to 6144 tokens, and together they fill all 8192 tokens.
All inputs are finite; a program needn't handle non-finite values.
Results may differ from a plain program's by a relative error of at most 0.019.
Values may be sent and summed in bfloat16 or wider, within the bound.
A program may use at most 64 MiB of HBM per device.

v0:
```python
import math
import jax
import jax.numpy as jnp
from jax import lax
from jax.sharding import PartitionSpec as P

QUERY_HEADS = 14
KEY_VALUE_HEADS = 2
HEAD_SIZE = 128
GROUP_SIZE = 7
BLK = 128
WB = 16


def passed_along(value, axis, steps):
    count = lax.axis_size(axis)
    first, last = (max(0, -steps), min(count, count - steps))
    return lax.ppermute(value, axis, [(source, source + steps) for source in range(first, last)])


def split_pack(packed_block):
    head_size_width = KEY_VALUE_HEADS * HEAD_SIZE
    key_head_rows = packed_block[:, :head_size_width].reshape(
        packed_block.shape[0], KEY_VALUE_HEADS, HEAD_SIZE
    )
    value_head_rows = packed_block[:, head_size_width:].reshape(
        packed_block.shape[0], KEY_VALUE_HEADS, HEAD_SIZE
    )
    return (key_head_rows, value_head_rows)


def local(query_in, key_in, value_input, output_gradient, doc_ids, query_bias):
    sharded_rows = query_in.shape[1]
    ctx_count = lax.axis_size("ctx")
    ctx_rank = lax.axis_index("ctx")
    score_scale = 1.0 / math.sqrt(HEAD_SIZE)
    blocks_here = sharded_rows // BLK
    window_slots = min((WB - 1 + blocks_here - 1) // blocks_here, ctx_count - 1) + 1
    group_slots = max(1, min(window_slots, 512 // sharded_rows))
    group_count = -(-window_slots // group_slots)
    padded_slots = group_count * group_slots
    grouped_rows = group_slots * sharded_rows
    packed_width = 2 * KEY_VALUE_HEADS * HEAD_SIZE
    query_rows = (query_in[0].astype(jnp.float32) + query_bias).astype(jnp.bfloat16)
    query_head_rows = query_rows.reshape(sharded_rows, KEY_VALUE_HEADS, GROUP_SIZE, HEAD_SIZE)
    gradient_heads = output_gradient[0].reshape(
        sharded_rows, KEY_VALUE_HEADS, GROUP_SIZE, HEAD_SIZE
    )
    own_pack = jnp.concatenate([key_in[0], value_input[0]], axis=1)
    own_docs = doc_ids[0]
    query_pos = ctx_rank * sharded_rows + jnp.arange(sharded_rows, dtype=jnp.int32)
    first_pack = jnp.concatenate(
        [own_pack[None], jnp.zeros((window_slots - 1, sharded_rows, packed_width), jnp.bfloat16)],
        axis=0,
    )
    first_docs = jnp.concatenate(
        [own_docs[None], jnp.zeros((window_slots - 1, sharded_rows), jnp.int32)], axis=0
    )

    def pass_on(step_index, running):
        stored_pack, stored_docs, moving_pack, moving_docs = running
        moving_pack, moving_docs = passed_along((moving_pack, moving_docs), "ctx", 1)
        stored_pack = lax.dynamic_update_index_in_dim(stored_pack, moving_pack, step_index, 0)
        stored_docs = lax.dynamic_update_index_in_dim(stored_docs, moving_docs, step_index, 0)
        return (stored_pack, stored_docs, moving_pack, moving_docs)

    window_pack, window_docs, _, _ = lax.fori_loop(
        1, window_slots, pass_on, (first_pack, first_docs, own_pack, own_docs)
    )
    spare_slots = padded_slots - window_slots
    window_pack = jnp.concatenate(
        [window_pack, jnp.zeros((spare_slots, sharded_rows, packed_width), jnp.bfloat16)], axis=0
    )
    window_pack = window_pack.reshape(group_count, grouped_rows, packed_width)
    window_docs = jnp.concatenate(
        [window_docs, jnp.zeros((spare_slots, sharded_rows), jnp.int32)], axis=0
    )
    window_docs = window_docs.reshape(group_count, grouped_rows)
    group_ids = jnp.arange(group_count, dtype=jnp.int32)

    def group_mask(group_index, docs_block):
        key_index = jnp.arange(grouped_rows, dtype=jnp.int32)
        slot_index = group_index * group_slots + key_index // sharded_rows
        key_pos = (ctx_rank - slot_index) * sharded_rows + key_index % sharded_rows
        inside = ((slot_index < window_slots) & (key_pos >= 0))[None, :]
        causal = key_pos[None, :] <= query_pos[:, None]
        near = query_pos[:, None] // BLK - key_pos[None, :] // BLK < WB
        same_doc = own_docs[:, None] == docs_block[None, :]
        return inside & causal & near & same_doc

    def group_scores(packed_block, allowed):
        key_head_rows, value_head_rows = split_pack(packed_block)
        scores = (
            jnp.einsum(
                "qgnd,kgd->gnqk", query_head_rows, key_head_rows, preferred_element_type=jnp.float32
            )
            * score_scale
        )
        return (jnp.where(allowed[None, None], scores, -jnp.inf), key_head_rows, value_head_rows)

    def forward_work(running, packed_block, allowed):
        row_max, row_sum, weighted = running
        scores, key_head_rows, value_head_rows = group_scores(packed_block, allowed)
        new_max = jnp.maximum(row_max, jnp.max(scores, axis=-1))
        rescale = jnp.exp(row_max - new_max)
        weights = jnp.exp(scores - new_max[..., None])
        row_sum = row_sum * rescale + jnp.sum(weights, axis=-1)
        weighted = weighted * rescale[..., None] + jnp.einsum(
            "gnqk,kgd->gnqd", weights, value_head_rows.astype(jnp.float32)
        )
        return (new_max, row_sum, weighted)

    def forward_step(running, inputs):
        packed_block, docs_block, group_index = inputs
        allowed = group_mask(group_index, docs_block)
        running = forward_work(running, packed_block, allowed)
        return (running, None)

    statistics_shape = (KEY_VALUE_HEADS, GROUP_SIZE, sharded_rows)
    start_stats = (
        jnp.full(statistics_shape, -jnp.inf, jnp.float32),
        jnp.zeros(statistics_shape, jnp.float32),
        jnp.zeros(statistics_shape + (HEAD_SIZE,), jnp.float32),
    )
    (row_max, row_sum, weighted), _ = lax.scan(
        forward_step, start_stats, (window_pack, window_docs, group_ids)
    )
    log_total = row_max + jnp.log(row_sum)
    attended = jnp.transpose(weighted / row_sum[..., None], (2, 0, 1, 3)).astype(jnp.bfloat16)
    row_dot = jnp.einsum(
        "qgnd,qgnd->gnq", gradient_heads, attended, preferred_element_type=jnp.float32
    )

    def backward_work(grad_query, packed_block, allowed):
        scores, key_head_rows, value_head_rows = group_scores(packed_block, allowed)
        attend = jnp.exp(scores - log_total[..., None])
        grad_prob = jnp.einsum(
            "qgnd,kgd->gnqk", gradient_heads, value_head_rows, preferred_element_type=jnp.float32
        )
        grad_score = (attend * (grad_prob - row_dot[..., None])).astype(jnp.bfloat16)
        grad_query = grad_query + jnp.einsum(
            "gnqk,kgd->qgnd", grad_score, key_head_rows, preferred_element_type=jnp.float32
        )
        key_gradient = (
            jnp.einsum(
                "gnqk,qgnd->kgd", grad_score, query_head_rows, preferred_element_type=jnp.float32
            )
            * score_scale
        )
        value_gradient = jnp.einsum(
            "gnqk,qgnd->kgd",
            attend.astype(jnp.bfloat16),
            gradient_heads,
            preferred_element_type=jnp.float32,
        )
        partial_value = jnp.concatenate(
            [
                key_gradient.reshape(grouped_rows, KEY_VALUE_HEADS * HEAD_SIZE),
                value_gradient.reshape(grouped_rows, KEY_VALUE_HEADS * HEAD_SIZE),
            ],
            axis=1,
        )
        return (grad_query, partial_value)

    def backward_step(grad_query, inputs):
        packed_block, docs_block, group_index = inputs
        allowed = group_mask(group_index, docs_block)
        return backward_work(grad_query, packed_block, allowed)

    grad_query, partials = lax.scan(
        backward_step,
        jnp.zeros((sharded_rows, KEY_VALUE_HEADS, GROUP_SIZE, HEAD_SIZE), jnp.float32),
        (window_pack, window_docs, group_ids),
    )
    partials = partials.reshape(padded_slots, sharded_rows, packed_width)
    query_grad = (grad_query * score_scale).reshape(sharded_rows, QUERY_HEADS * HEAD_SIZE)

    def return_partial(step_index, running):
        returned = passed_along(running, "ctx", -1)
        return returned + lax.dynamic_index_in_dim(
            partials, window_slots - 1 - step_index, 0, keepdims=False
        )

    summed_total = lax.fori_loop(1, window_slots, return_partial, partials[window_slots - 1])
    key_gradient = summed_total[:, : KEY_VALUE_HEADS * HEAD_SIZE].astype(jnp.bfloat16)
    value_gradient = summed_total[:, KEY_VALUE_HEADS * HEAD_SIZE :].astype(jnp.bfloat16)
    grad_bias = lax.psum(jnp.sum(query_grad, axis=0), ("dp", "ctx"))
    attended_out = attended.reshape(sharded_rows, QUERY_HEADS * HEAD_SIZE)
    return (
        attended_out[None],
        query_grad.astype(jnp.bfloat16)[None],
        key_gradient[None],
        value_gradient[None],
        grad_bias,
    )


def solution(mesh):
    placed = (
        P("dp", "ctx", None),
        P("dp", "ctx", None),
        P("dp", "ctx", None),
        P("dp", "ctx", None),
        P("dp", "ctx"),
        P(),
    )
    return jax.shard_map(
        local,
        mesh=mesh,
        in_specs=placed,
        out_specs=(
            P("dp", "ctx", None),
            P("dp", "ctx", None),
            P("dp", "ctx", None),
            P("dp", "ctx", None),
            P(),
        ),
        check_vma=False,
    )
```

profile of v0, /device:TPU:1, one launch (start us, length us, event | category | flops | bytes accessed | tf_op | source)
XLA Modules:
  0.0 563.7 jit_solution(16847469983181574787)
XLA Ops:
  8.9 138.4 %while.72 = (s32[]{:T(128)}, bf16[16,128,512]{2,1,0:T(8,128)(2,1)}, s32[16,128]{1,0:T(8,128)S(1)}, bf16[128,512]{1,0:T(8,128)(2,1)S(1)}, s32[128]{0:T(128)S(1)}, /*index=5*/s32[]{:T(128)}, s32[]{:T(128)}, s32[]{:T(128)}) while((s32[]{:T(128)}, bf16[16,128,512]{2,1,0:T(8,128)(2,1)}, s32[16,128]{1,0:T(8,128)S(1)}, ...), condition=%wide.region_1.2_spmd, body=%wide.region_0.1_spmd.sunk | while | flops 5 | bytes 1052879 | solution.py:67
  8.9 4.1 collective-permute-start
  29.2 4.8 collective-permute-start.1
  57.1 4.0 collective-permute-start.1
  66.1 4.0 collective-permute-start.1
  75.2 4.0 collective-permute-start.1
  84.2 4.0 collective-permute-start.1
  93.2 4.3 collective-permute-start.1
  102.5 4.8 collective-permute-start.1
  112.4 4.3 collective-permute-start.1
  131.0 4.5 collective-permute-start.1
  140.5 5.3 collective-permute-start.1
  147.3 4.1 copy.51
  151.5 23.1 %while.74 = (s32[]{:T(128)}, f32[2,7,128]{2,1,0:T(8,128)S(1)}, f32[2,7,128]{2,1,0:T(8,128)S(1)}, f32[2,7,128,128]{3,2,1,0:T(8,128)S(1)}, s32[4]{0:T(128)S(1)}, /...) while((s32[]{:T(128)}, f32[2,7,128]{2,1,0:T(8,128)S(1)}, ...), condition=%wide.region_5.6_spmd.clone.clone.clone, body=%wide.region_2.5_spmd.clone.clone.clone.sunk | while | flops 480120704 | bytes 16320205 | solution.py:125
  179.3 42.8 %while.75 = (s32[]{:T(128)}, f32[128,2,7,128]{0,3,2,1:T(8,128)S(1)}, f32[4,512,512]{2,1,0:T(8,128)}, bf16[4,512,512]{1,2,0:T(8,128)(2,1)}, s32[4]{0:T(128)S(1)},...) while((s32[]{:T(128)}, ...), condition=%wide.region_7.8_spmd.clone.clone.clone, body=%wide.region_6.7_spmd.clone.clone.clone.sunk | while | flops 1184918656 | bytes 30644960 | solution.py:170
  223.1 163.2 %while.73 = (s32[]{:T(128)}, f32[128,512]{1,0:T(8,128)S(1)}, f32[16,128,512]{2,1,0:T(8,128)}, s32[]{:T(128)}, s32[]{:T(128)}, /*index=5*/s32[]{:T(128)}, s32[]{:T(128)}) while((s32[]{:T(128)}, f32[128,512]{1,0:T(8,128)S(1)}, f32[16,128,512]{2,1,0:T(8,128)}, s32[]{:T(128)}, s32[]{:T(128)}, /*index=5*/s32[]{:T(128)}, s32[]{:T(128)}) %tuple.177), condition=%wide.region_9.10_spmd, body=%wide.region_8.9_spmd.sunk | while | flops 65542 | bytes 1835175 | solution.py:184
  224.4 6.0 %collective-permute-done.2 = f32[128,512]{1,0:T(8,128)S(1)} collective-permute-done((f32[128,512]{1,0:T(8,128)S(1)}, f32[128,512]{1,0:T(8,128)S(1)}, u32[]{:S(2)}, u32[]{:S(2)}) %collective-permute-start.2) | collective-permute-done | bytes 262176 | tf_op jit(solution)/shard_map/while/body/eval_jaxpr/ppermute | solution.py:18
  232.7 7.8 %collective-permute-done.2 = f32[128,512]{1,0:T(8,128)S(1)} collective-permute-done((f32[128,512]{1,0:T(8,128)S(1)}, f32[128,512]{1,0:T(8,128)S(1)}, u32[]{:S(2)}, u32[]{:S(2)}) %collective-permute-start.2) | collective-permute-done | bytes 262176 | tf_op jit(solution)/shard_map/while/body/eval_jaxpr/ppermute | solution.py:18
  242.8 7.7 %collective-permute-done.2 = f32[128,512]{1,0:T(8,128)S(1)} collective-permute-done((f32[128,512]{1,0:T(8,128)S(1)}, f32[128,512]{1,0:T(8,128)S(1)}, u32[]{:S(2)}, u32[]{:S(2)}) %collective-permute-start.2) | collective-permute-done | bytes 262176 | tf_op jit(solution)/shard_map/while/body/eval_jaxpr/ppermute | solution.py:18
  252.8 10.2 %collective-permute-done.2 = f32[128,512]{1,0:T(8,128)S(1)} collective-permute-done((f32[128,512]{1,0:T(8,128)S(1)}, f32[128,512]{1,0:T(8,128)S(1)}, u32[]{:S(2)}, u32[]{:S(2)}) %collective-permute-start.2) | collective-permute-done | bytes 262176 | tf_op jit(solution)/shard_map/while/body/eval_jaxpr/ppermute | solution.py:18
  265.3 11.4 %collective-permute-done.2 = f32[128,512]{1,0:T(8,128)S(1)} collective-permute-done((f32[128,512]{1,0:T(8,128)S(1)}, f32[128,512]{1,0:T(8,128)S(1)}, u32[]{:S(2)}, u32[]{:S(2)}) %collective-permute-start.2) | collective-permute-done | bytes 262176 | tf_op jit(solution)/shard_map/while/body/eval_jaxpr/ppermute | solution.py:18
  279.0 9.2 %collective-permute-done.2 = f32[128,512]{1,0:T(8,128)S(1)} collective-permute-done((f32[128,512]{1,0:T(8,128)S(1)}, f32[128,512]{1,0:T(8,128)S(1)}, u32[]{:S(2)}, u32[]{:S(2)}) %collective-permute-start.2) | collective-permute-done | bytes 262176 | tf_op jit(solution)/shard_map/while/body/eval_jaxpr/ppermute | solution.py:18
  290.5 7.4 %collective-permute-done.2 = f32[128,512]{1,0:T(8,128)S(1)} collective-permute-done((f32[128,512]{1,0:T(8,128)S(1)}, f32[128,512]{1,0:T(8,128)S(1)}, u32[]{:S(2)}, u32[]{:S(2)}) %collective-permute-start.2) | collective-permute-done | bytes 262176 | tf_op jit(solution)/shard_map/while/body/eval_jaxpr/ppermute | solution.py:18
  300.1 6.8 %collective-permute-done.2 = f32[128,512]{1,0:T(8,128)S(1)} collective-permute-done((f32[128,512]{1,0:T(8,128)S(1)}, f32[128,512]{1,0:T(8,128)S(1)}, u32[]{:S(2)}, u32[]{:S(2)}) %collective-permute-start.2) | collective-permute-done | bytes 262176 | tf_op jit(solution)/shard_map/while/body/eval_jaxpr/ppermute | solution.py:18
  309.3 7.6 %collective-permute-done.2 = f32[128,512]{1,0:T(8,128)S(1)} collective-permute-done((f32[128,512]{1,0:T(8,128)S(1)}, f32[128,512]{1,0:T(8,128)S(1)}, u32[]{:S(2)}, u32[]{:S(2)}) %collective-permute-start.2) | collective-permute-done | bytes 262176 | tf_op jit(solution)/shard_map/while/body/eval_jaxpr/ppermute | solution.py:18
  319.2 7.9 %collective-permute-done.2 = f32[128,512]{1,0:T(8,128)S(1)} collective-permute-done((f32[128,512]{1,0:T(8,128)S(1)}, f32[128,512]{1,0:T(8,128)S(1)}, u32[]{:S(2)}, u32[]{:S(2)}) %collective-permute-start.2) | collective-permute-done | bytes 262176 | tf_op jit(solution)/shard_map/while/body/eval_jaxpr/ppermute | solution.py:18
  329.4 7.9 %collective-permute-done.2 = f32[128,512]{1,0:T(8,128)S(1)} collective-permute-done((f32[128,512]{1,0:T(8,128)S(1)}, f32[128,512]{1,0:T(8,128)S(1)}, u32[]{:S(2)}, u32[]{:S(2)}) %collective-permute-start.2) | collective-permute-done | bytes 262176 | tf_op jit(solution)/shard_map/while/body/eval_jaxpr/ppermute | solution.py:18
  339.7 7.9 %collective-permute-done.2 = f32[128,512]{1,0:T(8,128)S(1)} collective-permute-done((f32[128,512]{1,0:T(8,128)S(1)}, f32[128,512]{1,0:T(8,128)S(1)}, u32[]{:S(2)}, u32[]{:S(2)}) %collective-permute-start.2) | collective-permute-done | bytes 262176 | tf_op jit(solution)/shard_map/while/body/eval_jaxpr/ppermute | solution.py:18
  349.9 8.8 %collective-permute-done.2 = f32[128,512]{1,0:T(8,128)S(1)} collective-permute-done((f32[128,512]{1,0:T(8,128)S(1)}, f32[128,512]{1,0:T(8,128)S(1)}, u32[]{:S(2)}, u32[]{:S(2)}) %collective-permute-start.2) | collective-permute-done | bytes 262176 | tf_op jit(solution)/shard_map/while/body/eval_jaxpr/ppermute | solution.py:18
  361.0 10.4 %collective-permute-done.2 = f32[128,512]{1,0:T(8,128)S(1)} collective-permute-done((f32[128,512]{1,0:T(8,128)S(1)}, f32[128,512]{1,0:T(8,128)S(1)}, u32[]{:S(2)}, u32[]{:S(2)}) %collective-permute-start.2) | collective-permute-done | bytes 262176 | tf_op jit(solution)/shard_map/while/body/eval_jaxpr/ppermute | solution.py:18
  373.7 11.5 %collective-permute-done.2 = f32[128,512]{1,0:T(8,128)S(1)} collective-permute-done((f32[128,512]{1,0:T(8,128)S(1)}, f32[128,512]{1,0:T(8,128)S(1)}, u32[]{:S(2)}, u32[]{:S(2)}) %collective-permute-start.2) | collective-permute-done | bytes 262176 | tf_op jit(solution)/shard_map/while/body/eval_jaxpr/ppermute | solution.py:18
  387.3 175.4 %psum.7 = f32[1792]{0:T(1024)} all-reduce(f32[1792]{0:T(1024)S(1)} %reduce_sum.25), channel_id=1, replica_groups=mesh['dp'=8,'ctx'=64] {'dp','ctx'}, use_global_device_ids=true, to_apply=%region_11.12 | all-reduce | flops 1792 | bytes 14336 | tf_op jit(solution)/shard_map/psum | solution.py:187
  (290 shorter events, 199.7 us)
Async XLA Ops:
  8.9 7.9 %collective-permute-start = (bf16[128,512]{1,0:T(8,128)(2,1)S(1)}, bf16[128,512]{1,0:T(8,128)(2,1)S(1)}, u32[]{:S(2)}, u32[]{:S(2)}) collective-permute-start(bf16[128,512]{1,0:T(8,128)(2,1)S(1)} %get-tuple-element.1222), channel_id=1, source_target_pairs={{0,1},{1,2},{2,3},{3,4},{4,5},{5,6},{6,7},{7,8},{8,9},{9,10},{10,1... | collective-permute-start | bytes 393224 | tf_op jit(solution)/shard_map/while/body/eval_jaxpr/ppermute | solution.py:18
  17.5 7.4 %collective-permute-start = (bf16[128,512]{1,0:T(8,128)(2,1)S(1)}, bf16[128,512]{1,0:T(8,128)(2,1)S(1)}, u32[]{:S(2)}, u32[]{:S(2)}) collective-permute-start(bf16[128,512]{1,0:T(8,128)(2,1)S(1)} %get-tuple-element.1222), channel_id=1, source_target_pairs={{0,1},{1,2},{2,3},{3,4},{4,5},{5,6},{6,7},{7,8},{8,9},{9,10},{10,1... | collective-permute-start | bytes 393224 | tf_op jit(solution)/shard_map/while/body/eval_jaxpr/ppermute | solution.py:18
  25.7 9.1 %collective-permute-start = (bf16[128,512]{1,0:T(8,128)(2,1)S(1)}, bf16[128,512]{1,0:T(8,128)(2,1)S(1)}, u32[]{:S(2)}, u32[]{:S(2)}) collective-permute-start(bf16[128,512]{1,0:T(8,128)(2,1)S(1)} %get-tuple-element.1222), channel_id=1, source_target_pairs={{0,1},{1,2},{2,3},{3,4},{4,5},{5,6},{6,7},{7,8},{8,9},{9,10},{10,1... | collective-permute-start | bytes 393224 | tf_op jit(solution)/shard_map/while/body/eval_jaxpr/ppermute | solution.py:18
  35.5 8.3 %collective-permute-start = (bf16[128,512]{1,0:T(8,128)(2,1)S(1)}, bf16[128,512]{1,0:T(8,128)(2,1)S(1)}, u32[]{:S(2)}, u32[]{:S(2)}) collective-permute-start(bf16[128,512]{1,0:T(8,128)(2,1)S(1)} %get-tuple-element.1222), channel_id=1, source_target_pairs={{0,1},{1,2},{2,3},{3,4},{4,5},{5,6},{6,7},{7,8},{8,9},{9,10},{10,1... | collective-permute-start | bytes 393224 | tf_op jit(solution)/shard_map/while/body/eval_jaxpr/ppermute | solution.py:18
  44.5 8.3 %collective-permute-start = (bf16[128,512]{1,0:T(8,128)(2,1)S(1)}, bf16[128,512]{1,0:T(8,128)(2,1)S(1)}, u32[]{:S(2)}, u32[]{:S(2)}) collective-permute-start(bf16[128,512]{1,0:T(8,128)(2,1)S(1)} %get-tuple-element.1222), channel_id=1, source_target_pairs={{0,1},{1,2},{2,3},{3,4},{4,5},{5,6},{6,7},{7,8},{8,9},{9,10},{10,1... | collective-permute-start | bytes 393224 | tf_op jit(solution)/shard_map/while/body/eval_jaxpr/ppermute | solution.py:18
  53.5 8.3 %collective-permute-start = (bf16[128,512]{1,0:T(8,128)(2,1)S(1)}, bf16[128,512]{1,0:T(8,128)(2,1)S(1)}, u32[]{:S(2)}, u32[]{:S(2)}) collective-permute-start(bf16[128,512]{1,0:T(8,128)(2,1)S(1)} %get-tuple-element.1222), channel_id=1, source_target_pairs={{0,1},{1,2},{2,3},{3,4},{4,5},{5,6},{6,7},{7,8},{8,9},{9,10},{10,1... | collective-permute-start | bytes 393224 | tf_op jit(solution)/shard_map/while/body/eval_jaxpr/ppermute | solution.py:18
  62.6 8.3 %collective-permute-start = (bf16[128,512]{1,0:T(8,128)(2,1)S(1)}, bf16[128,512]{1,0:T(8,128)(2,1)S(1)}, u32[]{:S(2)}, u32[]{:S(2)}) collective-permute-start(bf16[128,512]{1,0:T(8,128)(2,1)S(1)} %get-tuple-element.1222), channel_id=1, source_target_pairs={{0,1},{1,2},{2,3},{3,4},{4,5},{5,6},{6,7},{7,8},{8,9},{9,10},{10,1... | collective-permute-start | bytes 393224 | tf_op jit(solution)/shard_map/while/body/eval_jaxpr/ppermute | solution.py:18
  71.6 8.3 %collective-permute-start = (bf16[128,512]{1,0:T(8,128)(2,1)S(1)}, bf16[128,512]{1,0:T(8,128)(2,1)S(1)}, u32[]{:S(2)}, u32[]{:S(2)}) collective-permute-start(bf16[128,512]{1,0:T(8,128)(2,1)S(1)} %get-tuple-element.1222), channel_id=1, source_target_pairs={{0,1},{1,2},{2,3},{3,4},{4,5},{5,6},{6,7},{7,8},{8,9},{9,10},{10,1... | collective-permute-start | bytes 393224 | tf_op jit(solution)/shard_map/while/body/eval_jaxpr/ppermute | solution.py:18
  80.6 8.4 %collective-permute-start = (bf16[128,512]{1,0:T(8,128)(2,1)S(1)}, bf16[128,512]{1,0:T(8,128)(2,1)S(1)}, u32[]{:S(2)}, u32[]{:S(2)}) collective-permute-start(bf16[128,512]{1,0:T(8,128)(2,1)S(1)} %get-tuple-element.1222), channel_id=1, source_target_pairs={{0,1},{1,2},{2,3},{3,4},{4,5},{5,6},{6,7},{7,8},{8,9},{9,10},{10,1... | collective-permute-start | bytes 393224 | tf_op jit(solution)/shard_map/while/body/eval_jaxpr/ppermute | solution.py:18
  89.7 8.6 %collective-permute-start = (bf16[128,512]{1,0:T(8,128)(2,1)S(1)}, bf16[128,512]{1,0:T(8,128)(2,1)S(1)}, u32[]{:S(2)}, u32[]{:S(2)}) collective-permute-start(bf16[128,512]{1,0:T(8,128)(2,1)S(1)} %get-tuple-element.1222), channel_id=1, source_target_pairs={{0,1},{1,2},{2,3},{3,4},{4,5},{5,6},{6,7},{7,8},{8,9},{9,10},{10,1... | collective-permute-start | bytes 393224 | tf_op jit(solution)/shard_map/while/body/eval_jaxpr/ppermute | solution.py:18
  99.0 9.1 %collective-permute-start = (bf16[128,512]{1,0:T(8,128)(2,1)S(1)}, bf16[128,512]{1,0:T(8,128)(2,1)S(1)}, u32[]{:S(2)}, u32[]{:S(2)}) collective-permute-start(bf16[128,512]{1,0:T(8,128)(2,1)S(1)} %get-tuple-element.1222), channel_id=1, source_target_pairs={{0,1},{1,2},{2,3},{3,4},{4,5},{5,6},{6,7},{7,8},{8,9},{9,10},{10,1... | collective-permute-start | bytes 393224 | tf_op jit(solution)/shard_map/while/body/eval_jaxpr/ppermute | solution.py:18
  102.5 5.5 collective-permute-start.1
  108.8 8.6 %collective-permute-start = (bf16[128,512]{1,0:T(8,128)(2,1)S(1)}, bf16[128,512]{1,0:T(8,128)(2,1)S(1)}, u32[]{:S(2)}, u32[]{:S(2)}) collective-permute-start(bf16[128,512]{1,0:T(8,128)(2,1)S(1)} %get-tuple-element.1222), channel_id=1, source_target_pairs={{0,1},{1,2},{2,3},{3,4},{4,5},{5,6},{6,7},{7,8},{8,9},{9,10},{10,1... | collective-permute-start | bytes 393224 | tf_op jit(solution)/shard_map/while/body/eval_jaxpr/ppermute | solution.py:18
  118.1 8.3 %collective-permute-start = (bf16[128,512]{1,0:T(8,128)(2,1)S(1)}, bf16[128,512]{1,0:T(8,128)(2,1)S(1)}, u32[]{:S(2)}, u32[]{:S(2)}) collective-permute-start(bf16[128,512]{1,0:T(8,128)(2,1)S(1)} %get-tuple-element.1222), channel_id=1, source_target_pairs={{0,1},{1,2},{2,3},{3,4},{4,5},{5,6},{6,7},{7,8},{8,9},{9,10},{10,1... | collective-permute-start | bytes 393224 | tf_op jit(solution)/shard_map/while/body/eval_jaxpr/ppermute | solution.py:18
  127.1 9.1 %collective-permute-start = (bf16[128,512]{1,0:T(8,128)(2,1)S(1)}, bf16[128,512]{1,0:T(8,128)(2,1)S(1)}, u32[]{:S(2)}, u32[]{:S(2)}) collective-permute-start(bf16[128,512]{1,0:T(8,128)(2,1)S(1)} %get-tuple-element.1222), channel_id=1, source_target_pairs={{0,1},{1,2},{2,3},{3,4},{4,5},{5,6},{6,7},{7,8},{8,9},{9,10},{10,1... | collective-permute-start | bytes 393224 | tf_op jit(solution)/shard_map/while/body/eval_jaxpr/ppermute | solution.py:18
  137.0 9.7 %collective-permute-start = (bf16[128,512]{1,0:T(8,128)(2,1)S(1)}, bf16[128,512]{1,0:T(8,128)(2,1)S(1)}, u32[]{:S(2)}, u32[]{:S(2)}) collective-permute-start(bf16[128,512]{1,0:T(8,128)(2,1)S(1)} %get-tuple-element.1222), channel_id=1, source_target_pairs={{0,1},{1,2},{2,3},{3,4},{4,5},{5,6},{6,7},{7,8},{8,9},{9,10},{10,1... | collective-permute-start | bytes 393224 | tf_op jit(solution)/shard_map/while/body/eval_jaxpr/ppermute | solution.py:18
  140.5 6.1 %collective-permute-start.1 = (s32[128]{0:T(128)S(1)}, s32[128]{0:T(128)S(1)}, u32[]{:S(2)}, u32[]{:S(2)}) collective-permute-start(s32[128]{0:T(128)S(1)} %get-tuple-element.1223), channel_id=1, source_target_pairs={{0,1},{1,2},{2,3},{3,4},{4,5},{5,6},{6,7},{7,8},{8,9},{9,10},{10,1... | collective-permute-start | bytes 1544 | tf_op jit(solution)/shard_map/while/body/eval_jaxpr/ppermute | solution.py:18
  223.1 7.3 %collective-permute-start.2 = (f32[128,512]{1,0:T(8,128)S(1)}, f32[128,512]{1,0:T(8,128)S(1)}, u32[]{:S(2)}, u32[]{:S(2)}) collective-permute-start(f32[128,512]{1,0:T(8,128)S(1)} %get-tuple-element.1333), channel_id=1, source_target_pairs={{1,0},{2,1},{3,2},{4,3},{5,4},{6,5},{7,6},{8,7},{9,8},{10,9},{11,1... | collective-permute-start | bytes 786440 | tf_op jit(solution)/shard_map/while/body/eval_jaxpr/ppermute | solution.py:18
  231.4 9.1 %collective-permute-start.2 = (f32[128,512]{1,0:T(8,128)S(1)}, f32[128,512]{1,0:T(8,128)S(1)}, u32[]{:S(2)}, u32[]{:S(2)}) collective-permute-start(f32[128,512]{1,0:T(8,128)S(1)} %get-tuple-element.1333), channel_id=1, source_target_pairs={{1,0},{2,1},{3,2},{4,3},{5,4},{6,5},{7,6},{8,7},{9,8},{10,9},{11,1... | collective-permute-start | bytes 786440 | tf_op jit(solution)/shard_map/while/body/eval_jaxpr/ppermute | solution.py:18
  241.5 9.0 %collective-permute-start.2 = (f32[128,512]{1,0:T(8,128)S(1)}, f32[128,512]{1,0:T(8,128)S(1)}, u32[]{:S(2)}, u32[]{:S(2)}) collective-permute-start(f32[128,512]{1,0:T(8,128)S(1)} %get-tuple-element.1333), channel_id=1, source_target_pairs={{1,0},{2,1},{3,2},{4,3},{5,4},{6,5},{7,6},{8,7},{9,8},{10,9},{11,1... | collective-permute-start | bytes 786440 | tf_op jit(solution)/shard_map/while/body/eval_jaxpr/ppermute | solution.py:18
  251.5 11.5 %collective-permute-start.2 = (f32[128,512]{1,0:T(8,128)S(1)}, f32[128,512]{1,0:T(8,128)S(1)}, u32[]{:S(2)}, u32[]{:S(2)}) collective-permute-start(f32[128,512]{1,0:T(8,128)S(1)} %get-tuple-element.1333), channel_id=1, source_target_pairs={{1,0},{2,1},{3,2},{4,3},{5,4},{6,5},{7,6},{8,7},{9,8},{10,9},{11,1... | collective-permute-start | bytes 786440 | tf_op jit(solution)/shard_map/while/body/eval_jaxpr/ppermute | solution.py:18
  264.0 12.7 %collective-permute-start.2 = (f32[128,512]{1,0:T(8,128)S(1)}, f32[128,512]{1,0:T(8,128)S(1)}, u32[]{:S(2)}, u32[]{:S(2)}) collective-permute-start(f32[128,512]{1,0:T(8,128)S(1)} %get-tuple-element.1333), channel_id=1, source_target_pairs={{1,0},{2,1},{3,2},{4,3},{5,4},{6,5},{7,6},{8,7},{9,8},{10,9},{11,1... | collective-permute-start | bytes 786440 | tf_op jit(solution)/shard_map/while/body/eval_jaxpr/ppermute | solution.py:18
  277.7 10.5 %collective-permute-start.2 = (f32[128,512]{1,0:T(8,128)S(1)}, f32[128,512]{1,0:T(8,128)S(1)}, u32[]{:S(2)}, u32[]{:S(2)}) collective-permute-start(f32[128,512]{1,0:T(8,128)S(1)} %get-tuple-element.1333), channel_id=1, source_target_pairs={{1,0},{2,1},{3,2},{4,3},{5,4},{6,5},{7,6},{8,7},{9,8},{10,9},{11,1... | collective-permute-start | bytes 786440 | tf_op jit(solution)/shard_map/while/body/eval_jaxpr/ppermute | solution.py:18
  289.2 8.7 %collective-permute-start.2 = (f32[128,512]{1,0:T(8,128)S(1)}, f32[128,512]{1,0:T(8,128)S(1)}, u32[]{:S(2)}, u32[]{:S(2)}) collective-permute-start(f32[128,512]{1,0:T(8,128)S(1)} %get-tuple-element.1333), channel_id=1, source_target_pairs={{1,0},{2,1},{3,2},{4,3},{5,4},{6,5},{7,6},{8,7},{9,8},{10,9},{11,1... | collective-permute-start | bytes 786440 | tf_op jit(solution)/shard_map/while/body/eval_jaxpr/ppermute | solution.py:18
  298.8 8.1 %collective-permute-start.2 = (f32[128,512]{1,0:T(8,128)S(1)}, f32[128,512]{1,0:T(8,128)S(1)}, u32[]{:S(2)}, u32[]{:S(2)}) collective-permute-start(f32[128,512]{1,0:T(8,128)S(1)} %get-tuple-element.1333), channel_id=1, source_target_pairs={{1,0},{2,1},{3,2},{4,3},{5,4},{6,5},{7,6},{8,7},{9,8},{10,9},{11,1... | collective-permute-start | bytes 786440 | tf_op jit(solution)/shard_map/while/body/eval_jaxpr/ppermute | solution.py:18
  308.0 8.9 %collective-permute-start.2 = (f32[128,512]{1,0:T(8,128)S(1)}, f32[128,512]{1,0:T(8,128)S(1)}, u32[]{:S(2)}, u32[]{:S(2)}) collective-permute-start(f32[128,512]{1,0:T(8,128)S(1)} %get-tuple-element.1333), channel_id=1, source_target_pairs={{1,0},{2,1},{3,2},{4,3},{5,4},{6,5},{7,6},{8,7},{9,8},{10,9},{11,1... | collective-permute-start | bytes 786440 | tf_op jit(solution)/shard_map/while/body/eval_jaxpr/ppermute | solution.py:18
  317.9 9.2 %collective-permute-start.2 = (f32[128,512]{1,0:T(8,128)S(1)}, f32[128,512]{1,0:T(8,128)S(1)}, u32[]{:S(2)}, u32[]{:S(2)}) collective-permute-start(f32[128,512]{1,0:T(8,128)S(1)} %get-tuple-element.1333), channel_id=1, source_target_pairs={{1,0},{2,1},{3,2},{4,3},{5,4},{6,5},{7,6},{8,7},{9,8},{10,9},{11,1... | collective-permute-start | bytes 786440 | tf_op jit(solution)/shard_map/while/body/eval_jaxpr/ppermute | solution.py:18
  328.1 9.2 %collective-permute-start.2 = (f32[128,512]{1,0:T(8,128)S(1)}, f32[128,512]{1,0:T(8,128)S(1)}, u32[]{:S(2)}, u32[]{:S(2)}) collective-permute-start(f32[128,512]{1,0:T(8,128)S(1)} %get-tuple-element.1333), channel_id=1, source_target_pairs={{1,0},{2,1},{3,2},{4,3},{5,4},{6,5},{7,6},{8,7},{9,8},{10,9},{11,1... | collective-permute-start | bytes 786440 | tf_op jit(solution)/shard_map/while/body/eval_jaxpr/ppermute | solution.py:18
  338.4 9.2 %collective-permute-start.2 = (f32[128,512]{1,0:T(8,128)S(1)}, f32[128,512]{1,0:T(8,128)S(1)}, u32[]{:S(2)}, u32[]{:S(2)}) collective-permute-start(f32[128,512]{1,0:T(8,128)S(1)} %get-tuple-element.1333), channel_id=1, source_target_pairs={{1,0},{2,1},{3,2},{4,3},{5,4},{6,5},{7,6},{8,7},{9,8},{10,9},{11,1... | collective-permute-start | bytes 786440 | tf_op jit(solution)/shard_map/while/body/eval_jaxpr/ppermute | solution.py:18
  348.6 10.1 %collective-permute-start.2 = (f32[128,512]{1,0:T(8,128)S(1)}, f32[128,512]{1,0:T(8,128)S(1)}, u32[]{:S(2)}, u32[]{:S(2)}) collective-permute-start(f32[128,512]{1,0:T(8,128)S(1)} %get-tuple-element.1333), channel_id=1, source_target_pairs={{1,0},{2,1},{3,2},{4,3},{5,4},{6,5},{7,6},{8,7},{9,8},{10,9},{11,1... | collective-permute-start | bytes 786440 | tf_op jit(solution)/shard_map/while/body/eval_jaxpr/ppermute | solution.py:18
  359.7 11.7 %collective-permute-start.2 = (f32[128,512]{1,0:T(8,128)S(1)}, f32[128,512]{1,0:T(8,128)S(1)}, u32[]{:S(2)}, u32[]{:S(2)}) collective-permute-start(f32[128,512]{1,0:T(8,128)S(1)} %get-tuple-element.1333), channel_id=1, source_target_pairs={{1,0},{2,1},{3,2},{4,3},{5,4},{6,5},{7,6},{8,7},{9,8},{10,9},{11,1... | collective-permute-start | bytes 786440 | tf_op jit(solution)/shard_map/while/body/eval_jaxpr/ppermute | solution.py:18
  372.4 12.8 %collective-permute-start.2 = (f32[128,512]{1,0:T(8,128)S(1)}, f32[128,512]{1,0:T(8,128)S(1)}, u32[]{:S(2)}, u32[]{:S(2)}) collective-permute-start(f32[128,512]{1,0:T(8,128)S(1)} %get-tuple-element.1333), channel_id=1, source_target_pairs={{1,0},{2,1},{3,2},{4,3},{5,4},{6,5},{7,6},{8,7},{9,8},{10,9},{11,1... | collective-permute-start | bytes 786440 | tf_op jit(solution)/shard_map/while/body/eval_jaxpr/ppermute | solution.py:18
  (15 other events, 204.2 us)
where the time goes:
time: 567 us; the launch traced here: 564 us
  blocking collectives  175 us (31%)
  waiting for transfers between devices  139 us (25%)
  starting transfers between devices  136 us (24%)
  local copies, waits for them, and re-layouts  47.1 us (8%)
  matrix products  34.2 us (6%)
  other arithmetic  24 us (4%)
  loops' own time  6.87 us (1%)
    psum x1, blocking collectives, local(): grad_bias = lax.psum(jnp.sum(query_grad, axis=0), ('dp', 'ctx'))  175 us
    ppermute x45, waiting for transfers between devices, passed_along(): lax.ppermute(value, axis, [(source, source + steps) for source in range(f...  139 us
    ppermute x45, starting transfers between devices, passed_along(): lax.ppermute(value, axis, [(source, source + steps) for source in range(f...  136 us
    add x15, other arithmetic, return_partial(): returned + lax.dynamic_index_in_dim(partials, window_slots - 1 - step_ind...  14.8 us
  transfers between devices with their start and end apart: 45, of which 30 were waited for; matrix products, arithmetic and copies ran while one was open for 0% of the time, Pallas kernels for 0%

commit v1 on v0

--- a/solution.py
+++ b/solution.py
@@ -184,7 +184,7 @@
     summed_total = lax.fori_loop(1, window_slots, return_partial, partials[window_slots - 1])
     key_gradient = summed_total[:, : KEY_VALUE_HEADS * HEAD_SIZE].astype(jnp.bfloat16)
     value_gradient = summed_total[:, KEY_VALUE_HEADS * HEAD_SIZE :].astype(jnp.bfloat16)
-    grad_bias = lax.psum(jnp.sum(query_grad, axis=0), ("dp", "ctx"))
+    grad_bias = jnp.sum(lax.all_gather(jnp.sum(query_grad, axis=0), ("dp", "ctx")), axis=0)
     attended_out = attended.reshape(sharded_rows, QUERY_HEADS * HEAD_SIZE)
     return (
         attended_out[None],

time: 567 us -> 480 us (0.85)
  blocking collectives: 175 us -> 0 us
  waiting for transfers between devices: 139 us -> 208 us
  between operations: 0.74 us -> 14.2 us
    psum x1 -> x0, blocking collectives: 175 us -> none  [local(): grad_bias = lax.psum(jnp.sum(query_grad, axis=0), ('dp', 'ctx'))]
    all_gather x0 -> x1, waiting for transfers between devices: none -> 67.8 us  [local(): lax.all_gather(jnp.sum(query_grad, axis=0), ('dp', 'ctx'))]
  transfers between devices with their start and end apart: 45 -> 46, of which waited for: 30 -> 31; matrix products, arithmetic and copies ran while one was open for 0% -> 4% of each run, Pallas kernels for 0% -> 0%
where the time goes in v1:
time: 480 us; the launch traced here: 475 us
  waiting for transfers between devices  208 us (43%)
  starting transfers between devices  136 us (28%)
  local copies, waits for them, and re-layouts  46.7 us (10%)
  matrix products  34.2 us (7%)
  other arithmetic  28.5 us (6%)
  between operations  14.2 us (3%)
  loops' own time  6.8 us (1%)
    ppermute x45, waiting for transfers between devices, passed_along(): lax.ppermute(value, axis, [(source, source + steps) for source in range(f...  140 us
    ppermute x45, starting transfers between devices, passed_along(): lax.ppermute(value, axis, [(source, source + steps) for source in range(f...  136 us
    all_gather x1, waiting for transfers between devices, local(): lax.all_gather(jnp.sum(query_grad, axis=0), ('dp', 'ctx'))  67.8 us
    add x15, other arithmetic, return_partial(): returned + lax.dynamic_index_in_dim(partials, window_slots - 1 - step_ind...  14.8 us
    unnamed x13, local copies, waits for them, and re-layouts  10.7 us
    dynamic_update_slice x15, local copies, waits for them, and re-layouts, pass_on(): lax.dynamic_update_index_in_dim(stored_pack, moving_pack, step_index, 0)  10.1 us
  transfers between devices with their start and end apart: 46, of which 31 were waited for; matrix products, arithmetic and copies ran while one was open for 4% of the time, Pallas kernels for 0%

profile of v1, /device:TPU:1, one launch (start us, length us, event | category | flops | bytes accessed | tf_op | source)
XLA Modules:
  0.0 474.8 jit_solution(14726019425262697306)
XLA Ops:
  14.7 138.4 %while.72 = (s32[]{:T(128)}, bf16[16,128,512]{2,1,0:T(8,128)(2,1)}, s32[16,128]{1,0:T(8,128)S(1)}, bf16[128,512]{1,0:T(8,128)(2,1)S(1)}, s32[128]{0:T(128)S(1)}, /*index=5*/s32[]{:T(128)}, s32[]{:T(128)}, s32[]{:T(128)}) while((s32[]{:T(128)}, bf16[16,128,512]{2,1,0:T(8,128)(2,1)}, s32[16,128]{1,0:T(8,128)S(1)}, ...), condition=%wide.region_1.2_spmd, body=%wide.region_0.1_spmd.sunk | while | flops 5 | bytes 1052879 | solution.py:67
  14.7 4.1 collective-permute-start
  35.0 4.8 %collective-permute-start.1 = (s32[128]{0:T(128)S(1)}, s32[128]{0:T(128)S(1)}, u32[]{:S(2)}, u32[]{:S(2)}) collective-permute-start(s32[128]{0:T(128)S(1)} %get-tuple-element.1252), channel_id=1, source_target_pairs={{0,1},{1,2},{2,3},{3,4},{4,5},{5,6},{6,7},{7,8},{8,9},{9,10},{10,1... | collective-permute-start | bytes 1544 | tf_op jit(solution)/shard_map/while/body/eval_jaxpr/ppermute | solution.py:18
  62.9 4.0 collective-permute-start.1
  71.9 4.0 collective-permute-start.1
  90.0 4.0 collective-permute-start.1
  99.1 4.3 collective-permute-start.1
  108.3 4.8 %collective-permute-start.1 = (s32[128]{0:T(128)S(1)}, s32[128]{0:T(128)S(1)}, u32[]{:S(2)}, u32[]{:S(2)}) collective-permute-start(s32[128]{0:T(128)S(1)} %get-tuple-element.1252), channel_id=1, source_target_pairs={{0,1},{1,2},{2,3},{3,4},{4,5},{5,6},{6,7},{7,8},{8,9},{9,10},{10,1... | collective-permute-start | bytes 1544 | tf_op jit(solution)/shard_map/while/body/eval_jaxpr/ppermute | solution.py:18
  118.2 4.3 collective-permute-start.1
  136.8 4.5 collective-permute-start.1
  146.3 5.3 %collective-permute-start.1 = (s32[128]{0:T(128)S(1)}, s32[128]{0:T(128)S(1)}, u32[]{:S(2)}, u32[]{:S(2)}) collective-permute-start(s32[128]{0:T(128)S(1)} %get-tuple-element.1252), channel_id=1, source_target_pairs={{0,1},{1,2},{2,3},{3,4},{4,5},{5,6},{6,7},{7,8},{8,9},{9,10},{10,1... | collective-permute-start | bytes 1544 | tf_op jit(solution)/shard_map/while/body/eval_jaxpr/ppermute | solution.py:18
  153.1 4.1 copy.70
  157.3 23.1 %while.74 = (s32[]{:T(128)}, f32[2,7,128]{2,1,0:T(8,128)S(1)}, f32[2,7,128]{2,1,0:T(8,128)S(1)}, f32[2,7,128,128]{3,2,1,0:T(8,128)S(1)}, s32[4]{0:T(128)S(1)}, /...) while((s32[]{:T(128)}, f32[2,7,128]{2,1,0:T(8,128)S(1)}, ...), condition=%wide.region_5.6_spmd.clone.clone.clone, body=%wide.region_2.5_spmd.clone.clone.clone.sunk | while | flops 480120704 | bytes 16320205 | solution.py:125
  182.7 42.8 %while.75 = (s32[]{:T(128)}, f32[128,2,7,128]{0,3,2,1:T(8,128)S(1)}, f32[4,512,512]{2,1,0:T(8,128)}, bf16[4,512,512]{1,2,0:T(8,128)(2,1)}, s32[4]{0:T(128)S(1)},...) while((s32[]{:T(128)}, ...), condition=%wide.region_7.8_spmd.clone.clone.clone, body=%wide.region_6.7_spmd.clone.clone.clone.sunk | while | flops 1184918656 | bytes 30644960 | solution.py:170
  229.5 164.4 %while.73 = (s32[]{:T(128)}, f32[128,512]{1,0:T(8,128)S(1)}, f32[16,128,512]{2,1,0:T(8,128)}, s32[]{:T(128)}, s32[]{:T(128)}, /*index=5*/s32[]{:T(128)}, s32[]{:T(128)}) while((s32[]{:T(128)}, f32[128,512]{1,0:T(8,128)S(1)}, f32[16,128,512]{2,1,0:T(8,128)}, s32[]{:T(128)}, s32[]{:T(128)}, /*index=5*/s32[]{:T(128)}, s32[]{:T(128)}) %tuple.182), condition=%wide.region_9.10_spmd, body=%wide.region_8.9_spmd.sunk | while | flops 65542 | bytes 1835175 | solution.py:184
  230.8 6.0 %collective-permute-done.2 = f32[128,512]{1,0:T(8,128)S(1)} collective-permute-done((f32[128,512]{1,0:T(8,128)S(1)}, f32[128,512]{1,0:T(8,128)S(1)}, u32[]{:S(2)}, u32[]{:S(2)}) %collective-permute-start.2) | collective-permute-done | bytes 262176 | tf_op jit(solution)/shard_map/while/body/eval_jaxpr/ppermute | solution.py:18
  239.1 7.8 %collective-permute-done.2 = f32[128,512]{1,0:T(8,128)S(1)} collective-permute-done((f32[128,512]{1,0:T(8,128)S(1)}, f32[128,512]{1,0:T(8,128)S(1)}, u32[]{:S(2)}, u32[]{:S(2)}) %collective-permute-start.2) | collective-permute-done | bytes 262176 | tf_op jit(solution)/shard_map/while/body/eval_jaxpr/ppermute | solution.py:18
  249.2 7.7 %collective-permute-done.2 = f32[128,512]{1,0:T(8,128)S(1)} collective-permute-done((f32[128,512]{1,0:T(8,128)S(1)}, f32[128,512]{1,0:T(8,128)S(1)}, u32[]{:S(2)}, u32[]{:S(2)}) %collective-permute-start.2) | collective-permute-done | bytes 262176 | tf_op jit(solution)/shard_map/while/body/eval_jaxpr/ppermute | solution.py:18
  259.2 10.2 %collective-permute-done.2 = f32[128,512]{1,0:T(8,128)S(1)} collective-permute-done((f32[128,512]{1,0:T(8,128)S(1)}, f32[128,512]{1,0:T(8,128)S(1)}, u32[]{:S(2)}, u32[]{:S(2)}) %collective-permute-start.2) | collective-permute-done | bytes 262176 | tf_op jit(solution)/shard_map/while/body/eval_jaxpr/ppermute | solution.py:18
  271.7 11.4 %collective-permute-done.2 = f32[128,512]{1,0:T(8,128)S(1)} collective-permute-done((f32[128,512]{1,0:T(8,128)S(1)}, f32[128,512]{1,0:T(8,128)S(1)}, u32[]{:S(2)}, u32[]{:S(2)}) %collective-permute-start.2) | collective-permute-done | bytes 262176 | tf_op jit(solution)/shard_map/while/body/eval_jaxpr/ppermute | solution.py:18
  285.4 9.1 %collective-permute-done.2 = f32[128,512]{1,0:T(8,128)S(1)} collective-permute-done((f32[128,512]{1,0:T(8,128)S(1)}, f32[128,512]{1,0:T(8,128)S(1)}, u32[]{:S(2)}, u32[]{:S(2)}) %collective-permute-start.2) | collective-permute-done | bytes 262176 | tf_op jit(solution)/shard_map/while/body/eval_jaxpr/ppermute | solution.py:18
  296.9 7.8 %collective-permute-done.2 = f32[128,512]{1,0:T(8,128)S(1)} collective-permute-done((f32[128,512]{1,0:T(8,128)S(1)}, f32[128,512]{1,0:T(8,128)S(1)}, u32[]{:S(2)}, u32[]{:S(2)}) %collective-permute-start.2) | collective-permute-done | bytes 262176 | tf_op jit(solution)/shard_map/while/body/eval_jaxpr/ppermute | solution.py:18
  306.9 6.9 %collective-permute-done.2 = f32[128,512]{1,0:T(8,128)S(1)} collective-permute-done((f32[128,512]{1,0:T(8,128)S(1)}, f32[128,512]{1,0:T(8,128)S(1)}, u32[]{:S(2)}, u32[]{:S(2)}) %collective-permute-start.2) | collective-permute-done | bytes 262176 | tf_op jit(solution)/shard_map/while/body/eval_jaxpr/ppermute | solution.py:18
  316.1 7.7 %collective-permute-done.2 = f32[128,512]{1,0:T(8,128)S(1)} collective-permute-done((f32[128,512]{1,0:T(8,128)S(1)}, f32[128,512]{1,0:T(8,128)S(1)}, u32[]{:S(2)}, u32[]{:S(2)}) %collective-permute-start.2) | collective-permute-done | bytes 262176 | tf_op jit(solution)/shard_map/while/body/eval_jaxpr/ppermute | solution.py:18
  326.1 7.9 %collective-permute-done.2 = f32[128,512]{1,0:T(8,128)S(1)} collective-permute-done((f32[128,512]{1,0:T(8,128)S(1)}, f32[128,512]{1,0:T(8,128)S(1)}, u32[]{:S(2)}, u32[]{:S(2)}) %collective-permute-start.2) | collective-permute-done | bytes 262176 | tf_op jit(solution)/shard_map/while/body/eval_jaxpr/ppermute | solution.py:18
  336.4 8.0 %collective-permute-done.2 = f32[128,512]{1,0:T(8,128)S(1)} collective-permute-done((f32[128,512]{1,0:T(8,128)S(1)}, f32[128,512]{1,0:T(8,128)S(1)}, u32[]{:S(2)}, u32[]{:S(2)}) %collective-permute-start.2) | collective-permute-done | bytes 262176 | tf_op jit(solution)/shard_map/while/body/eval_jaxpr/ppermute | solution.py:18
  346.6 8.3 %collective-permute-done.2 = f32[128,512]{1,0:T(8,128)S(1)} collective-permute-done((f32[128,512]{1,0:T(8,128)S(1)}, f32[128,512]{1,0:T(8,128)S(1)}, u32[]{:S(2)}, u32[]{:S(2)}) %collective-permute-start.2) | collective-permute-done | bytes 262176 | tf_op jit(solution)/shard_map/while/body/eval_jaxpr/ppermute | solution.py:18
  357.2 8.6 %collective-permute-done.2 = f32[128,512]{1,0:T(8,128)S(1)} collective-permute-done((f32[128,512]{1,0:T(8,128)S(1)}, f32[128,512]{1,0:T(8,128)S(1)}, u32[]{:S(2)}, u32[]{:S(2)}) %collective-permute-start.2) | collective-permute-done | bytes 262176 | tf_op jit(solution)/shard_map/while/body/eval_jaxpr/ppermute | solution.py:18
  368.1 9.9 %collective-permute-done.2 = f32[128,512]{1,0:T(8,128)S(1)} collective-permute-done((f32[128,512]{1,0:T(8,128)S(1)}, f32[128,512]{1,0:T(8,128)S(1)}, u32[]{:S(2)}, u32[]{:S(2)}) %collective-permute-start.2) | collective-permute-done | bytes 262176 | tf_op jit(solution)/shard_map/while/body/eval_jaxpr/ppermute | solution.py:18
  380.3 12.5 %collective-permute-done.2 = f32[128,512]{1,0:T(8,128)S(1)} collective-permute-done((f32[128,512]{1,0:T(8,128)S(1)}, f32[128,512]{1,0:T(8,128)S(1)}, u32[]{:S(2)}, u32[]{:S(2)}) %collective-permute-start.2) | collective-permute-done | bytes 262176 | tf_op jit(solution)/shard_map/while/body/eval_jaxpr/ppermute | solution.py:18
  395.5 67.8 %all-gather.3.cloned.1.call-done = f32[512,1,1792]{2,1,0:T(1,128)} async-done(((f32[1,1,1792]{2,1,0:T(1,128)}), f32[512,1,1792]{2,1,0:T(1,128)}) %all-gather.3.cloned.1.call-update) | async-done | bytes 3670032 | tf_op jit(solution)/shard_map/all_gather | solution.py:187
  463.3 4.6 reduce_sum.32
  (295 shorter events, 203.2 us)
Async XLA Ops:
  7.2 456.1 %all-gather.3.cloned.1.call-start = ((), (), s32[]{:S(2)}) async-start(), calls=%async_computation | async-start | bytes 3677184 | tf_op jit(solution)/shard_map/all_gather | solution.py:187
  14.7 7.9 %collective-permute-start = (bf16[128,512]{1,0:T(8,128)(2,1)S(1)}, bf16[128,512]{1,0:T(8,128)(2,1)S(1)}, u32[]{:S(2)}, u32[]{:S(2)}) collective-permute-start(bf16[128,512]{1,0:T(8,128)(2,1)S(1)} %get-tuple-element.1251), channel_id=1, source_target_pairs={{0,1},{1,2},{2,3},{3,4},{4,5},{5,6},{6,7},{7,8},{8,9},{9,10},{10,1... | collective-permute-start | bytes 393224 | tf_op jit(solution)/shard_map/while/body/eval_jaxpr/ppermute | solution.py:18
  23.3 7.4 %collective-permute-start = (bf16[128,512]{1,0:T(8,128)(2,1)S(1)}, bf16[128,512]{1,0:T(8,128)(2,1)S(1)}, u32[]{:S(2)}, u32[]{:S(2)}) collective-permute-start(bf16[128,512]{1,0:T(8,128)(2,1)S(1)} %get-tuple-element.1251), channel_id=1, source_target_pairs={{0,1},{1,2},{2,3},{3,4},{4,5},{5,6},{6,7},{7,8},{8,9},{9,10},{10,1... | collective-permute-start | bytes 393224 | tf_op jit(solution)/shard_map/while/body/eval_jaxpr/ppermute | solution.py:18
  31.4 9.1 %collective-permute-start = (bf16[128,512]{1,0:T(8,128)(2,1)S(1)}, bf16[128,512]{1,0:T(8,128)(2,1)S(1)}, u32[]{:S(2)}, u32[]{:S(2)}) collective-permute-start(bf16[128,512]{1,0:T(8,128)(2,1)S(1)} %get-tuple-element.1251), channel_id=1, source_target_pairs={{0,1},{1,2},{2,3},{3,4},{4,5},{5,6},{6,7},{7,8},{8,9},{9,10},{10,1... | collective-permute-start | bytes 393224 | tf_op jit(solution)/shard_map/while/body/eval_jaxpr/ppermute | solution.py:18
  41.3 8.3 %collective-permute-start = (bf16[128,512]{1,0:T(8,128)(2,1)S(1)}, bf16[128,512]{1,0:T(8,128)(2,1)S(1)}, u32[]{:S(2)}, u32[]{:S(2)}) collective-permute-start(bf16[128,512]{1,0:T(8,128)(2,1)S(1)} %get-tuple-element.1251), channel_id=1, source_target_pairs={{0,1},{1,2},{2,3},{3,4},{4,5},{5,6},{6,7},{7,8},{8,9},{9,10},{10,1... | collective-permute-start | bytes 393224 | tf_op jit(solution)/shard_map/while/body/eval_jaxpr/ppermute | solution.py:18
  50.3 8.3 %collective-permute-start = (bf16[128,512]{1,0:T(8,128)(2,1)S(1)}, bf16[128,512]{1,0:T(8,128)(2,1)S(1)}, u32[]{:S(2)}, u32[]{:S(2)}) collective-permute-start(bf16[128,512]{1,0:T(8,128)(2,1)S(1)} %get-tuple-element.1251), channel_id=1, source_target_pairs={{0,1},{1,2},{2,3},{3,4},{4,5},{5,6},{6,7},{7,8},{8,9},{9,10},{10,1... | collective-permute-start | bytes 393224 | tf_op jit(solution)/shard_map/while/body/eval_jaxpr/ppermute | solution.py:18
  59.3 8.3 %collective-permute-start = (bf16[128,512]{1,0:T(8,128)(2,1)S(1)}, bf16[128,512]{1,0:T(8,128)(2,1)S(1)}, u32[]{:S(2)}, u32[]{:S(2)}) collective-permute-start(bf16[128,512]{1,0:T(8,128)(2,1)S(1)} %get-tuple-element.1251), channel_id=1, source_target_pairs={{0,1},{1,2},{2,3},{3,4},{4,5},{5,6},{6,7},{7,8},{8,9},{9,10},{10,1... | collective-permute-start | bytes 393224 | tf_op jit(solution)/shard_map/while/body/eval_jaxpr/ppermute | solution.py:18
  68.4 8.3 %collective-permute-start = (bf16[128,512]{1,0:T(8,128)(2,1)S(1)}, bf16[128,512]{1,0:T(8,128)(2,1)S(1)}, u32[]{:S(2)}, u32[]{:S(2)}) collective-permute-start(bf16[128,512]{1,0:T(8,128)(2,1)S(1)} %get-tuple-element.1251), channel_id=1, source_target_pairs={{0,1},{1,2},{2,3},{3,4},{4,5},{5,6},{6,7},{7,8},{8,9},{9,10},{10,1... | collective-permute-start | bytes 393224 | tf_op jit(solution)/shard_map/while/body/eval_jaxpr/ppermute | solution.py:18
  77.4 8.3 %collective-permute-start = (bf16[128,512]{1,0:T(8,128)(2,1)S(1)}, bf16[128,512]{1,0:T(8,128)(2,1)S(1)}, u32[]{:S(2)}, u32[]{:S(2)}) collective-permute-start(bf16[128,512]{1,0:T(8,128)(2,1)S(1)} %get-tuple-element.1251), channel_id=1, source_target_pairs={{0,1},{1,2},{2,3},{3,4},{4,5},{5,6},{6,7},{7,8},{8,9},{9,10},{10,1... | collective-permute-start | bytes 393224 | tf_op jit(solution)/shard_map/while/body/eval_jaxpr/ppermute | solution.py:18
  86.4 8.4 %collective-permute-start = (bf16[128,512]{1,0:T(8,128)(2,1)S(1)}, bf16[128,512]{1,0:T(8,128)(2,1)S(1)}, u32[]{:S(2)}, u32[]{:S(2)}) collective-permute-start(bf16[128,512]{1,0:T(8,128)(2,1)S(1)} %get-tuple-element.1251), channel_id=1, source_target_pairs={{0,1},{1,2},{2,3},{3,4},{4,5},{5,6},{6,7},{7,8},{8,9},{9,10},{10,1... | collective-permute-start | bytes 393224 | tf_op jit(solution)/shard_map/while/body/eval_jaxpr/ppermute | solution.py:18
  95.5 8.6 %collective-permute-start = (bf16[128,512]{1,0:T(8,128)(2,1)S(1)}, bf16[128,512]{1,0:T(8,128)(2,1)S(1)}, u32[]{:S(2)}, u32[]{:S(2)}) collective-permute-start(bf16[128,512]{1,0:T(8,128)(2,1)S(1)} %get-tuple-element.1251), channel_id=1, source_target_pairs={{0,1},{1,2},{2,3},{3,4},{4,5},{5,6},{6,7},{7,8},{8,9},{9,10},{10,1... | collective-permute-start | bytes 393224 | tf_op jit(solution)/shard_map/while/body/eval_jaxpr/ppermute | solution.py:18
  104.7 9.1 %collective-permute-start = (bf16[128,512]{1,0:T(8,128)(2,1)S(1)}, bf16[128,512]{1,0:T(8,128)(2,1)S(1)}, u32[]{:S(2)}, u32[]{:S(2)}) collective-permute-start(bf16[128,512]{1,0:T(8,128)(2,1)S(1)} %get-tuple-element.1251), channel_id=1, source_target_pairs={{0,1},{1,2},{2,3},{3,4},{4,5},{5,6},{6,7},{7,8},{8,9},{9,10},{10,1... | collective-permute-start | bytes 393224 | tf_op jit(solution)/shard_map/while/body/eval_jaxpr/ppermute | solution.py:18
  114.6 8.6 %collective-permute-start = (bf16[128,512]{1,0:T(8,128)(2,1)S(1)}, bf16[128,512]{1,0:T(8,128)(2,1)S(1)}, u32[]{:S(2)}, u32[]{:S(2)}) collective-permute-start(bf16[128,512]{1,0:T(8,128)(2,1)S(1)} %get-tuple-element.1251), channel_id=1, source_target_pairs={{0,1},{1,2},{2,3},{3,4},{4,5},{5,6},{6,7},{7,8},{8,9},{9,10},{10,1... | collective-permute-start | bytes 393224 | tf_op jit(solution)/shard_map/while/body/eval_jaxpr/ppermute | solution.py:18
  123.9 8.3 %collective-permute-start = (bf16[128,512]{1,0:T(8,128)(2,1)S(1)}, bf16[128,512]{1,0:T(8,128)(2,1)S(1)}, u32[]{:S(2)}, u32[]{:S(2)}) collective-permute-start(bf16[128,512]{1,0:T(8,128)(2,1)S(1)} %get-tuple-element.1251), channel_id=1, source_target_pairs={{0,1},{1,2},{2,3},{3,4},{4,5},{5,6},{6,7},{7,8},{8,9},{9,10},{10,1... | collective-permute-start | bytes 393224 | tf_op jit(solution)/shard_map/while/body/eval_jaxpr/ppermute | solution.py:18
  132.9 9.1 %collective-permute-start = (bf16[128,512]{1,0:T(8,128)(2,1)S(1)}, bf16[128,512]{1,0:T(8,128)(2,1)S(1)}, u32[]{:S(2)}, u32[]{:S(2)}) collective-permute-start(bf16[128,512]{1,0:T(8,128)(2,1)S(1)} %get-tuple-element.1251), channel_id=1, source_target_pairs={{0,1},{1,2},{2,3},{3,4},{4,5},{5,6},{6,7},{7,8},{8,9},{9,10},{10,1... | collective-permute-start | bytes 393224 | tf_op jit(solution)/shard_map/while/body/eval_jaxpr/ppermute | solution.py:18
  142.8 9.7 %collective-permute-start = (bf16[128,512]{1,0:T(8,128)(2,1)S(1)}, bf16[128,512]{1,0:T(8,128)(2,1)S(1)}, u32[]{:S(2)}, u32[]{:S(2)}) collective-permute-start(bf16[128,512]{1,0:T(8,128)(2,1)S(1)} %get-tuple-element.1251), channel_id=1, source_target_pairs={{0,1},{1,2},{2,3},{3,4},{4,5},{5,6},{6,7},{7,8},{8,9},{9,10},{10,1... | collective-permute-start | bytes 393224 | tf_op jit(solution)/shard_map/while/body/eval_jaxpr/ppermute | solution.py:18
  146.3 6.0 %collective-permute-start.1 = (s32[128]{0:T(128)S(1)}, s32[128]{0:T(128)S(1)}, u32[]{:S(2)}, u32[]{:S(2)}) collective-permute-start(s32[128]{0:T(128)S(1)} %get-tuple-element.1252), channel_id=1, source_target_pairs={{0,1},{1,2},{2,3},{3,4},{4,5},{5,6},{6,7},{7,8},{8,9},{9,10},{10,1... | collective-permute-start | bytes 1544 | tf_op jit(solution)/shard_map/while/body/eval_jaxpr/ppermute | solution.py:18
  229.5 7.3 %collective-permute-start.2 = (f32[128,512]{1,0:T(8,128)S(1)}, f32[128,512]{1,0:T(8,128)S(1)}, u32[]{:S(2)}, u32[]{:S(2)}) collective-permute-start(f32[128,512]{1,0:T(8,128)S(1)} %get-tuple-element.1362), channel_id=1, source_target_pairs={{1,0},{2,1},{3,2},{4,3},{5,4},{6,5},{7,6},{8,7},{9,8},{10,9},{11,1... | collective-permute-start | bytes 786440 | tf_op jit(solution)/shard_map/while/body/eval_jaxpr/ppermute | solution.py:18
  237.8 9.1 %collective-permute-start.2 = (f32[128,512]{1,0:T(8,128)S(1)}, f32[128,512]{1,0:T(8,128)S(1)}, u32[]{:S(2)}, u32[]{:S(2)}) collective-permute-start(f32[128,512]{1,0:T(8,128)S(1)} %get-tuple-element.1362), channel_id=1, source_target_pairs={{1,0},{2,1},{3,2},{4,3},{5,4},{6,5},{7,6},{8,7},{9,8},{10,9},{11,1... | collective-permute-start | bytes 786440 | tf_op jit(solution)/shard_map/while/body/eval_jaxpr/ppermute | solution.py:18
  247.9 9.0 %collective-permute-start.2 = (f32[128,512]{1,0:T(8,128)S(1)}, f32[128,512]{1,0:T(8,128)S(1)}, u32[]{:S(2)}, u32[]{:S(2)}) collective-permute-start(f32[128,512]{1,0:T(8,128)S(1)} %get-tuple-element.1362), channel_id=1, source_target_pairs={{1,0},{2,1},{3,2},{4,3},{5,4},{6,5},{7,6},{8,7},{9,8},{10,9},{11,1... | collective-permute-start | bytes 786440 | tf_op jit(solution)/shard_map/while/body/eval_jaxpr/ppermute | solution.py:18
  257.9 11.5 %collective-permute-start.2 = (f32[128,512]{1,0:T(8,128)S(1)}, f32[128,512]{1,0:T(8,128)S(1)}, u32[]{:S(2)}, u32[]{:S(2)}) collective-permute-start(f32[128,512]{1,0:T(8,128)S(1)} %get-tuple-element.1362), channel_id=1, source_target_pairs={{1,0},{2,1},{3,2},{4,3},{5,4},{6,5},{7,6},{8,7},{9,8},{10,9},{11,1... | collective-permute-start | bytes 786440 | tf_op jit(solution)/shard_map/while/body/eval_jaxpr/ppermute | solution.py:18
  270.4 12.7 %collective-permute-start.2 = (f32[128,512]{1,0:T(8,128)S(1)}, f32[128,512]{1,0:T(8,128)S(1)}, u32[]{:S(2)}, u32[]{:S(2)}) collective-permute-start(f32[128,512]{1,0:T(8,128)S(1)} %get-tuple-element.1362), channel_id=1, source_target_pairs={{1,0},{2,1},{3,2},{4,3},{5,4},{6,5},{7,6},{8,7},{9,8},{10,9},{11,1... | collective-permute-start | bytes 786440 | tf_op jit(solution)/shard_map/while/body/eval_jaxpr/ppermute | solution.py:18
  284.1 10.4 %collective-permute-start.2 = (f32[128,512]{1,0:T(8,128)S(1)}, f32[128,512]{1,0:T(8,128)S(1)}, u32[]{:S(2)}, u32[]{:S(2)}) collective-permute-start(f32[128,512]{1,0:T(8,128)S(1)} %get-tuple-element.1362), channel_id=1, source_target_pairs={{1,0},{2,1},{3,2},{4,3},{5,4},{6,5},{7,6},{8,7},{9,8},{10,9},{11,1... | collective-permute-start | bytes 786440 | tf_op jit(solution)/shard_map/while/body/eval_jaxpr/ppermute | solution.py:18
  295.5 9.1 %collective-permute-start.2 = (f32[128,512]{1,0:T(8,128)S(1)}, f32[128,512]{1,0:T(8,128)S(1)}, u32[]{:S(2)}, u32[]{:S(2)}) collective-permute-start(f32[128,512]{1,0:T(8,128)S(1)} %get-tuple-element.1362), channel_id=1, source_target_pairs={{1,0},{2,1},{3,2},{4,3},{5,4},{6,5},{7,6},{8,7},{9,8},{10,9},{11,1... | collective-permute-start | bytes 786440 | tf_op jit(solution)/shard_map/while/body/eval_jaxpr/ppermute | solution.py:18
  305.6 8.2 %collective-permute-start.2 = (f32[128,512]{1,0:T(8,128)S(1)}, f32[128,512]{1,0:T(8,128)S(1)}, u32[]{:S(2)}, u32[]{:S(2)}) collective-permute-start(f32[128,512]{1,0:T(8,128)S(1)} %get-tuple-element.1362), channel_id=1, source_target_pairs={{1,0},{2,1},{3,2},{4,3},{5,4},{6,5},{7,6},{8,7},{9,8},{10,9},{11,1... | collective-permute-start | bytes 786440 | tf_op jit(solution)/shard_map/while/body/eval_jaxpr/ppermute | solution.py:18
  314.8 9.0 %collective-permute-start.2 = (f32[128,512]{1,0:T(8,128)S(1)}, f32[128,512]{1,0:T(8,128)S(1)}, u32[]{:S(2)}, u32[]{:S(2)}) collective-permute-start(f32[128,512]{1,0:T(8,128)S(1)} %get-tuple-element.1362), channel_id=1, source_target_pairs={{1,0},{2,1},{3,2},{4,3},{5,4},{6,5},{7,6},{8,7},{9,8},{10,9},{11,1... | collective-permute-start | bytes 786440 | tf_op jit(solution)/shard_map/while/body/eval_jaxpr/ppermute | solution.py:18
  324.8 9.2 %collective-permute-start.2 = (f32[128,512]{1,0:T(8,128)S(1)}, f32[128,512]{1,0:T(8,128)S(1)}, u32[]{:S(2)}, u32[]{:S(2)}) collective-permute-start(f32[128,512]{1,0:T(8,128)S(1)} %get-tuple-element.1362), channel_id=1, source_target_pairs={{1,0},{2,1},{3,2},{4,3},{5,4},{6,5},{7,6},{8,7},{9,8},{10,9},{11,1... | collective-permute-start | bytes 786440 | tf_op jit(solution)/shard_map/while/body/eval_jaxpr/ppermute | solution.py:18
  335.1 9.3 %collective-permute-start.2 = (f32[128,512]{1,0:T(8,128)S(1)}, f32[128,512]{1,0:T(8,128)S(1)}, u32[]{:S(2)}, u32[]{:S(2)}) collective-permute-start(f32[128,512]{1,0:T(8,128)S(1)} %get-tuple-element.1362), channel_id=1, source_target_pairs={{1,0},{2,1},{3,2},{4,3},{5,4},{6,5},{7,6},{8,7},{9,8},{10,9},{11,1... | collective-permute-start | bytes 786440 | tf_op jit(solution)/shard_map/while/body/eval_jaxpr/ppermute | solution.py:18
  345.3 9.6 %collective-permute-start.2 = (f32[128,512]{1,0:T(8,128)S(1)}, f32[128,512]{1,0:T(8,128)S(1)}, u32[]{:S(2)}, u32[]{:S(2)}) collective-permute-start(f32[128,512]{1,0:T(8,128)S(1)} %get-tuple-element.1362), channel_id=1, source_target_pairs={{1,0},{2,1},{3,2},{4,3},{5,4},{6,5},{7,6},{8,7},{9,8},{10,9},{11,1... | collective-permute-start | bytes 786440 | tf_op jit(solution)/shard_map/while/body/eval_jaxpr/ppermute | solution.py:18
  355.9 9.9 %collective-permute-start.2 = (f32[128,512]{1,0:T(8,128)S(1)}, f32[128,512]{1,0:T(8,128)S(1)}, u32[]{:S(2)}, u32[]{:S(2)}) collective-permute-start(f32[128,512]{1,0:T(8,128)S(1)} %get-tuple-element.1362), channel_id=1, source_target_pairs={{1,0},{2,1},{3,2},{4,3},{5,4},{6,5},{7,6},{8,7},{9,8},{10,9},{11,1... | collective-permute-start | bytes 786440 | tf_op jit(solution)/shard_map/while/body/eval_jaxpr/ppermute | solution.py:18
  366.8 11.2 %collective-permute-start.2 = (f32[128,512]{1,0:T(8,128)S(1)}, f32[128,512]{1,0:T(8,128)S(1)}, u32[]{:S(2)}, u32[]{:S(2)}) collective-permute-start(f32[128,512]{1,0:T(8,128)S(1)} %get-tuple-element.1362), channel_id=1, source_target_pairs={{1,0},{2,1},{3,2},{4,3},{5,4},{6,5},{7,6},{8,7},{9,8},{10,9},{11,1... | collective-permute-start | bytes 786440 | tf_op jit(solution)/shard_map/while/body/eval_jaxpr/ppermute | solution.py:18
  379.0 13.8 %collective-permute-start.2 = (f32[128,512]{1,0:T(8,128)S(1)}, f32[128,512]{1,0:T(8,128)S(1)}, u32[]{:S(2)}, u32[]{:S(2)}) collective-permute-start(f32[128,512]{1,0:T(8,128)S(1)} %get-tuple-element.1362), channel_id=1, source_target_pairs={{1,0},{2,1},{3,2},{4,3},{5,4},{6,5},{7,6},{8,7},{9,8},{10,9},{11,1... | collective-permute-start | bytes 786440 | tf_op jit(solution)/shard_map/while/body/eval_jaxpr/ppermute | solution.py:18
  (17 other events, 220.6 us)
Sparse Core Ops, SparseCore 0:
  226.6 236.6 all-gather.2
